TPU v7x, 256 devices: a whole 4x4x8 slice. The times are simulated.
256 devices in a mesh: dp: 4 (over x), expert: 64 (over y, z, core).
Axes of the slice: x: 4, y: 4, z: 8, core: 2. Of those that a mesh axis runs over, the one named last changes fastest.
Arguments:
- tokens: bfloat16 [8192, 2048], P('expert'), may hold values from -4 to 4
- norm_gain: bfloat16 [2048], replicated, may hold values from 0.5 to 1.5
- routing_projection_matrix: bfloat16 [2048, 64], replicated, may hold values from -0.125 to 0.125
- experts: int32 [8192, 8], P('expert'), may hold values from 0 to 63, as said below
- replica_key: int32 [8192, 8], P('expert'), may hold values from 0 to 1048575
- slot_expert: int32 [128], replicated, may hold values from 0 to 63, as said below
- capacity: int32 [128], replicated, may hold values from 4 to 16, as said below
- slot_gate_up_weight: bfloat16 [128, 2048, 2, 1024], P('expert', None, None, 'dp'), may hold values from -0.125 to 0.125
- down_weight: bfloat16 [128, 1024, 2048], P('expert', 'dp'), may hold values from -0.1875 to 0.1875
Outputs:
- mixed: bfloat16 [8192, 2048], P('expert', 'dp')
Inputs may be any that keep to these rules, and one draw needn't show every extreme that they name: Each row names 8 different experts. `slot_expert`: every expert occupies at least one slot. `capacity`: for every j the capacities of slots 2 * j and 2 * j + 1 sum to at most 24, and to exactly 24 for some j.
All inputs are finite; a program needn't handle non-finite values.
Results may differ from a plain program's by a relative error of at most 0.012.
Values may be sent and summed in bfloat16 or wider, within the bound.
A program may use at most 128 MiB of HBM per device.

v0:
```python
import jax
import jax.numpy as jnp
from jax import lax
from jax.sharding import PartitionSpec as P

CAPACITY_HIGH = 16
CAP_DEV = 24


def assign_slots(experts, replica_key, slot_expert):
    flat_experts = experts.reshape(-1)
    holders = (flat_experts[:, None] == slot_expert[None, :]).astype(jnp.int32)
    copies = jnp.sum(holders, axis=1)
    earlier = jnp.cumsum(holders, axis=1) - holders
    wanted = replica_key.reshape(-1) % copies
    matched = holders * (earlier == wanted[:, None]).astype(jnp.int32)
    numbers = jnp.arange(slot_expert.shape[0], dtype=jnp.int32)
    return jnp.sum(matched * numbers[None, :], axis=1)


def slot_partial(flat_rows, gate_up_one, down_one):
    model_width = flat_rows.shape[1]
    unit_count = gate_up_one.shape[2]
    gate_up_out = jnp.dot(
        flat_rows,
        gate_up_one.reshape(model_width, 2 * unit_count),
        preferred_element_type=jnp.float32,
    )
    activated = (jax.nn.silu(gate_up_out[:, :unit_count]) * gate_up_out[:, unit_count:]).astype(
        jnp.bfloat16
    )
    result = jnp.dot(activated, down_one, preferred_element_type=jnp.float32)
    return result.astype(jnp.bfloat16)


def on_device(
    tokens,
    norm_gain,
    routing_projection_matrix,
    experts,
    replica_key,
    slot_expert,
    capacity,
    slot_gate_up_weight,
    down_weight,
):
    peer_count = lax.axis_size("expert")
    group_count = lax.axis_size("dp")
    group_pos = lax.axis_index("dp")
    me = lax.axis_index("expert")
    rows_here = tokens.shape[0]
    model_width = tokens.shape[1]
    pick_count = experts.shape[1]
    slot_count = slot_expert.shape[0]
    per_device = slot_count // peer_count
    quarter = model_width // group_count
    buffer_rows = CAP_DEV
    hidden = tokens.astype(jnp.float32)
    scale = lax.rsqrt(jnp.mean(hidden * hidden, axis=-1, keepdims=True) + 1e-06)
    normed = (hidden * scale * norm_gain.astype(jnp.float32)).astype(jnp.bfloat16)
    logits = jnp.dot(normed, routing_projection_matrix, preferred_element_type=jnp.float32)
    score = jax.nn.sigmoid(jnp.take_along_axis(logits, experts, axis=1)).reshape(-1)
    slot_ids = assign_slots(experts, replica_key, slot_expert)
    onehot = (slot_ids[:, None] == jnp.arange(slot_count, dtype=jnp.int32)[None, :]).astype(
        jnp.int32
    )
    position = jnp.sum((jnp.cumsum(onehot, axis=0) - onehot) * onehot, axis=1)
    slot_cap = jnp.sum(onehot * capacity[None, :], axis=1)
    kept_mask = position < slot_cap
    is_second = slot_ids % per_device == 1
    row_in = jnp.where(is_second, buffer_rows - slot_cap + position, position)
    target = jnp.where(
        kept_mask, slot_ids // per_device * buffer_rows + row_in, peer_count * buffer_rows
    )
    source_rows = jnp.arange(rows_here * pick_count, dtype=jnp.int32) // pick_count
    normed_part = lax.dynamic_slice_in_dim(normed, group_pos * quarter, quarter, 1)
    outgoing = (
        jnp.zeros((peer_count * buffer_rows + 1, quarter), jnp.bfloat16)
        .at[target]
        .set(normed_part[source_rows])
    )
    outgoing = outgoing[:-1].reshape(peer_count, buffer_rows, quarter)
    incoming_part = lax.all_to_all(outgoing, "expert", split_axis=0, concat_axis=0, tiled=True)
    incoming = lax.all_gather(incoming_part, "dp", axis=2, tiled=True)
    flat_in = incoming.reshape(peer_count * buffer_rows, model_width)
    first_out = slot_partial(flat_in, slot_gate_up_weight[0], down_weight[0])
    second_out = slot_partial(flat_in, slot_gate_up_weight[1], down_weight[1])
    first_cap = lax.dynamic_index_in_dim(capacity, me * per_device, keepdims=False)
    row_index = jnp.arange(peer_count * buffer_rows, dtype=jnp.int32) % buffer_rows
    partial_value = jnp.where((row_index < first_cap)[:, None], first_out, second_out)
    partial_value = partial_value.reshape(peer_count, buffer_rows, model_width)
    summed = lax.psum_scatter(partial_value, "dp", scatter_dimension=2, tiled=True)
    returned = lax.all_to_all(summed, "expert", split_axis=0, concat_axis=0, tiled=True)
    flat_ret = returned.reshape(peer_count * buffer_rows, quarter)
    flat_ret = jnp.concatenate([flat_ret, jnp.zeros((1, quarter), flat_ret.dtype)])
    weight_kept = jnp.where(kept_mask, score, jnp.float32(0.0))
    gathered = flat_ret[target].astype(jnp.float32).reshape(rows_here, pick_count, quarter)
    mixture = jnp.sum(weight_kept.reshape(rows_here, pick_count)[:, :, None] * gathered, axis=1)
    residual = lax.dynamic_slice_in_dim(tokens, group_pos * quarter, quarter, 1).astype(jnp.float32)
    return (residual + mixture).astype(jnp.bfloat16)


def solution(mesh):
    in_specs = (
        P("expert", None),
        P(),
        P(),
        P("expert", None),
        P("expert", None),
        P(),
        P(),
        P("expert", None, None, "dp"),
        P("expert", "dp", None),
    )
    out_specs = P("expert", "dp")
    return jax.shard_map(
        on_device, mesh=mesh, in_specs=in_specs, out_specs=out_specs, check_vma=False
    )
```

profile of v0, /device:TPU:1, one launch (start us, length us, event | category | flops | bytes accessed | tf_op | source)
XLA Modules:
  0.0 289.3 jit_solution(4413022350040989855)
XLA Ops:
  6.6 0.8 copy.21
  7.5 0.8 convert_reduce_fusion
  8.3 0.8 compare_convert_fusion
  9.0 1.2 fusion.3
  10.3 0.7 convert_element_type.50
  11.0 0.8 copy.22
  14.4 10.1 %scatter_custom_fusion = bf16[1537,512]{1,0:T(8,128)(2,1)S(1)} fusion(s32[1024]{0:T(1024)S(1)} %bitcast.69, bf16[128,512]{1,0:T(8,128)(2,1)S(1)} %constant_dynamic-slice_fusion, s32[1024]{0:T(1024)S(1)} %broadcast_clamp_fusion.1, bf16[]{:T(256)} %constant.114.clone.1), kind=kCustom, calls=%fused_computation.20 | custom fusion | bytes 1573890 | tf_op jit(solution)/shard_map/scatter | solution.py:80
  24.6 52.9 %all_to_all.10 = bf16[64,24,512]{2,1,0:T(8,128)(2,1)} all-to-all(bf16[64,24,512]{2,1,0:T(8,128)(2,1)S(1)} %bitcast.59), channel_id=1, replica_groups=mesh['dp'=4,'expert'=64] {'expert'}, dimensions={0} | all-to-all | bytes 3145728 | tf_op jit(solution)/shard_map/all_to_all | solution.py:83
  77.7 0.6 dynamic_slice.11
  78.3 4.7 %fusion.32 = (bf16[1,2048,2,256]{3,2,1,0:T(2,128)(2,1)S(1)}, bf16[1,2048,2,256]{3,2,1,0:T(2,128)(2,1)S(1)}) fusion(bf16[2,2048,2,256]{3,2,1,0:T(2,128)(2,1)} %param.16), kind=kLoop, calls=%fused_computation.77 | loop fusion | bytes 8388608 | tf_op jit(solution)/shard_map/slice | solution.py:86
  83.5 1.8 copy.31
  85.4 0.7 fusion.26
  86.0 56.6 %all-gather.2.cloned.1.call-done = bf16[64,24,2048]{2,1,0:T(8,128)(2,1)} async-done(((bf16[64,24,512]{2,1,0:T(8,128)(2,1)}), bf16[64,24,2048]{2,1,0:T(8,128)(2,1)}) %all-gather.2.cloned.1.call-update) | async-done | bytes 6291472 | tf_op jit(solution)/shard_map/all_gather | solution.py:84
  142.6 6.3 %fusion.35 = f32[1536,512]{1,0:T(8,128)S(1)} fusion(bf16[1536,2048]{1,0:T(8,128)(2,1)} %bitcast.71, bf16[2048,512]{1,0:T(8,128)(2,1)} %bitcast.62), kind=kOutput, calls=%fused_computation.80 | convolution fusion | flops 3221225472 | bytes 11534336 | tf_op jit(solution)/shard_map/dot_general | solution.py:24
  148.9 3.5 %fusion.34 = f32[1536,512]{1,0:T(8,128)S(1)} fusion(bf16[1536,2048]{1,0:T(8,128)(2,1)S(1)} %bitcast.72, bf16[2048,512]{1,0:T(8,128)(2,1)S(1)} %bitcast.61), kind=kOutput, calls=%fused_computation.79 | convolution fusion | flops 3221225472 | bytes 11534336 | tf_op jit(solution)/shard_map/dot_general | solution.py:24
  152.4 1.9 convolution_convert_fusion
  154.3 3.9 %broadcast_select_fusion = bf16[1536,2048]{1,0:T(8,128)(2,1)} fusion(bf16[1536,2048]{1,0:T(8,128)(2,1)S(1)} %convolution_convert_fusion, pred[1536]{0:T(1024)(128)(4,1)S(1)} %fusion.26, bf16[2,256,2048]{2,1,0:T(8,128)(2,1)S(1)} %copy-done.8, f32[1536,512]{1,0:T(8,128)S(1)} %fusion.34), kind=kOutput, calls=%fused_computation.6 | convolution fusion | flops 1619263488 | bytes 16779264 | tf_op jit(solution)/shard_map/dot_general | solution.py:32
  158.3 67.4 %reduce-scatter.2.cloned.1.call-done = bf16[64,24,512]{2,1,0:T(8,128)(2,1)} async-done(((bf16[64,24,2048]{2,1,0:T(8,128)(2,1)}), bf16[64,24,512]{2,1,0:T(8,128)(2,1)}) %reduce-scatter.2.cloned.1.call-update) | async-done | bytes 1572880 | tf_op jit(solution)/shard_map/reduce_scatter | solution.py:92
  225.7 10.6 %all-to-all-start.1 = ((bf16[64,24,512]{2,1,0:T(8,128)(2,1)}), bf16[64,24,512]{2,1,0:T(8,128)(2,1)S(1)}, u32[]{:S(2)}, u32[]{:S(2)}) async-start(bf16[64,24,512]{2,1,0:T(8,128)(2,1)} %reduce-scatter.2.cloned.1.call-done), calls=%async_computation.2 | async-start | bytes 3145728 | tf_op jit(solution)/shard_map/all_to_all | solution.py:93
  236.9 7.0 %gather_fusion.1 = f32[1024]{0:T(1024)S(1)} fusion(f32[128,64]{0,1:T(8,128)S(1)} %fusion.33, s32[1024]{0:T(1024)S(1)} %reshape.274), kind=kCustom, calls=%fused_computation.2 | custom fusion | bytes 16384 | tf_op jit(solution)/shard_map/jit(take_along_axis)/gather | solution.py:62
  244.4 31.7 %all-to-all-done.1 = bf16[64,24,512]{2,1,0:T(8,128)(2,1)S(1)} async-done(((bf16[64,24,512]{2,1,0:T(8,128)(2,1)}), bf16[64,24,512]{2,1,0:T(8,128)(2,1)S(1)}, u32[]{:S(2)}, u32[]{:S(2)}) %all-to-all-start.1) | async-done | bytes 1572896 | tf_op jit(solution)/shard_map/all_to_all | solution.py:93
  276.2 4.0 %gather_fusion = bf16[1024,512]{1,0:T(8,128)(2,1)S(1)} fusion(bf16[1537,512]{1,0:T(8,128)(2,1)S(1)} %concatenate.3, s32[1024]{0:T(1024)S(1)} %broadcast_clamp_fusion), kind=kCustom, calls=%fused_computation.1 | custom fusion | bytes 2101248 | tf_op jit(solution)/shard_map/gather | solution.py:97
  280.2 0.7 fusion
  280.9 1.6 add_convert_fusion
  (56 shorter events, 4.5 us)
Async XLA Ops:
  6.5 230.0 %copy-start = (bf16[2048,64]{0,1:T(8,128)(2,1)S(1)}, bf16[2048,64]{0,1:T(8,128)(2,1)}, u32[]{:S(2)}) copy-start(bf16[2048,64]{0,1:T(8,128)(2,1)} %param.11) | copy-start | bytes 786436
  6.5 5.9 %copy-start.5 = (s32[128]{0:T(128)S(1)}, s32[128]{0:T(128)}, u32[]{:S(2)}) copy-start(s32[128]{0:T(128)} %param.14) | copy-start | bytes 1540
  6.5 136.1 %all-gather.2.cloned.1.call-start = ((), (), s32[]{:S(2)}) async-start(), calls=%async_computation.3 | async-start | bytes 7864320 | tf_op jit(solution)/shard_map/all_gather | solution.py:84
  11.9 1.5 copy-start.1
  12.7 0.9 copy-start.6
  13.6 0.8 copy-start.2
  77.5 148.1 %reduce-scatter.2.cloned.1.call-start = ((), (), s32[]{:S(2)}) async-start(), calls=%async_computation.4 | async-start | bytes 7864320 | tf_op jit(solution)/shard_map/reduce_scatter | solution.py:92
  142.6 6.3 %copy-start.7 = (bf16[64,24,2048]{2,1,0:T(8,128)(2,1)S(1)}, bf16[64,24,2048]{2,1,0:T(8,128)(2,1)}, u32[]{:S(2)}) copy-start(bf16[64,24,2048]{2,1,0:T(8,128)(2,1)} %all-gather.2.cloned.1.call-done) | copy-start | bytes 18874372
  148.9 3.5 %copy-start.8 = (bf16[2,256,2048]{2,1,0:T(8,128)(2,1)S(1)}, bf16[2,256,2048]{2,1,0:T(8,128)(2,1)}, u32[]{:S(2)}) copy-start(bf16[2,256,2048]{2,1,0:T(8,128)(2,1)} %param.17) | copy-start | bytes 6291460
  158.2 78.1 %copy-start.4 = (s32[128,8]{0,1:T(8,128)S(1)}, s32[128,8]{0,1:T(8,128)}, u32[]{:S(2)}) copy-start(s32[128,8]{0,1:T(8,128)} %param.12) | copy-start | bytes 12292
  158.3 78.3 %copy-start.3 = (bf16[128,2048]{1,0:T(8,128)(2,1)S(1)}, bf16[128,2048]{1,0:T(8,128)(2,1)}, u32[]{:S(2)}) copy-start(bf16[128,2048]{1,0:T(8,128)(2,1)} %copy-done.2) | copy-start | bytes 1572868
  225.7 50.4 %all-to-all-start.1 = ((bf16[64,24,512]{2,1,0:T(8,128)(2,1)}), bf16[64,24,512]{2,1,0:T(8,128)(2,1)S(1)}, u32[]{:S(2)}, u32[]{:S(2)}) async-start(bf16[64,24,512]{2,1,0:T(8,128)(2,1)} %reduce-scatter.2.cloned.1.call-done), calls=%async_computation.2 | async-start | bytes 3145728 | tf_op jit(solution)/shard_map/all_to_all | solution.py:93
Sparse Core Ops, SparseCore 0:
  77.6 64.9 all-gather.1
  158.4 67.2 reduce-scatter.1
where the time goes:
time: 290 us; the launch traced here: 289 us
  waiting for transfers between devices  156 us (54%)
  blocking collectives  52.9 us (18%)
  local copies, waits for them, and re-layouts  32.3 us (11%)
  matrix products  15.8 us (5%)
  between operations  13.8 us (5%)
  starting transfers between devices  10.9 us (4%)
  other arithmetic  7.97 us (3%)
    reduce_scatter x1, waiting for transfers between devices, on_device(): lax.psum_scatter(partial_value, 'dp', scatter_dimension=2, tiled=True)  67.4 us
    all_gather x1, waiting for transfers between devices, on_device(): incoming = lax.all_gather(incoming_part, 'dp', axis=2, tiled=True)  56.6 us
    all_to_all x1, blocking collectives, on_device(): lax.all_to_all(outgoing, 'expert', split_axis=0, concat_axis=0, tiled=True)  52.9 us
    all_to_all x1, waiting for transfers between devices, on_device(): lax.all_to_all(summed, 'expert', split_axis=0, concat_axis=0, tiled=True)  31.7 us
    all_to_all x1, starting transfers between devices, on_device(): lax.all_to_all(summed, 'expert', split_axis=0, concat_axis=0, tiled=True)  10.6 us
    scatter x1, local copies, waits for them, and re-layouts, on_device(): outgoing = jnp.zeros((peer_count * buffer_rows + 1, quarter), jnp.bfloat1...  10.1 us
    dot_general x2, matrix products, slot_partial(): jnp.dot(flat_rows, gate_up_one.reshape(model_width, 2 * unit_count), pref...  9.76 us
    gather x5, local copies, waits for them, and re-layouts, on_device(): jnp.take_along_axis(logits, experts, axis=1)  7.34 us
  transfers between devices with their start and end apart: 3, of which 3 were waited for; matrix products, arithmetic and copies ran while one was open for 6% of the time, Pallas kernels for 0%

commit v1 on v0

--- a/solution.py
+++ b/solution.py
@@ -81,7 +81,8 @@
     )
     outgoing = outgoing[:-1].reshape(peer_count, buffer_rows, quarter)
     incoming_part = lax.all_to_all(outgoing, "expert", split_axis=0, concat_axis=0, tiled=True)
-    incoming = lax.all_gather(incoming_part, "dp", axis=2, tiled=True)
+    sent = jnp.stack([incoming_part] * lax.axis_size("dp"))
+    incoming = jnp.concatenate(lax.all_to_all(sent, "dp", 0, 0), axis=2)
     flat_in = incoming.reshape(peer_count * buffer_rows, model_width)
     first_out = slot_partial(flat_in, slot_gate_up_weight[0], down_weight[0])
     second_out = slot_partial(flat_in, slot_gate_up_weight[1], down_weight[1])

time: 290 us -> 310 us (1.069)
  local copies, waits for them, and re-layouts: 32.3 us -> 50.8 us
  starting transfers between devices: 10.9 us -> 15.9 us
    all_to_all x0 -> x1, waiting for transfers between devices: none -> 61.4 us  [on_device(): incoming = jnp.concatenate(lax.all_to_all(sent, 'dp', 0, 0), axis=2)]
    all_gather x1 -> x0, waiting for transfers between devices: 56.6 us -> none  [on_device(): incoming = lax.all_gather(incoming_part, 'dp', axis=2, tiled=True)]
    reshape x0 -> x1, local copies, waits for them, and re-layouts: none -> 10.9 us  [on_device(): incoming = jnp.concatenate(lax.all_to_all(sent, 'dp', 0, 0), axis=2)]
    reduce_scatter x1, waiting for transfers between devices: 67.4 us -> 61.9 us  [on_device(): lax.psum_scatter(partial_value, 'dp', scatter_dimension=2, tiled=True)]
    all_to_all x0 -> x1, starting transfers between devices: none -> 5.24 us  [on_device(): incoming = jnp.concatenate(lax.all_to_all(sent, 'dp', 0, 0), axis=2)]
    unnamed x22 -> x25, local copies, waits for them, and re-layouts: 4.48 us -> 8.83 us
    another operation x3 -> x4, local copies, waits for them, and re-layouts: 0.28 us -> 3.45 us  [the longest x1 3.17 us: on_device(): sent = jnp.stack([incoming_part] * lax.axis_size('dp'))]
where the time goes in v1:
time: 310 us; the launch traced here: 309 us
  waiting for transfers between devices  155 us (50%)
  blocking collectives  52.7 us (17%)
  local copies, waits for them, and re-layouts  50.8 us (16%)
  starting transfers between devices  15.9 us (5%)
  between operations  13.8 us (4%)
  matrix products  13.1 us (4%)
  other arithmetic  7.97 us (3%)
    reduce_scatter x1, waiting for transfers between devices, on_device(): lax.psum_scatter(partial_value, 'dp', scatter_dimension=2, tiled=True)  61.9 us
    all_to_all x1, waiting for transfers between devices, on_device(): incoming = jnp.concatenate(lax.all_to_all(sent, 'dp', 0, 0), axis=2)  61.4 us
    all_to_all x1, blocking collectives, on_device(): lax.all_to_all(outgoing, 'expert', split_axis=0, concat_axis=0, tiled=True)  52.7 us
    all_to_all x1, waiting for transfers between devices, on_device(): lax.all_to_all(summed, 'expert', split_axis=0, concat_axis=0, tiled=True)  31.7 us
    reshape x1, local copies, waits for them, and re-layouts, on_device(): incoming = jnp.concatenate(lax.all_to_all(sent, 'dp', 0, 0), axis=2)  10.9 us
    all_to_all x1, starting transfers between devices, on_device(): lax.all_to_all(summed, 'expert', split_axis=0, concat_axis=0, tiled=True)  10.6 us
    scatter x1, local copies, waits for them, and re-layouts, on_device(): outgoing = jnp.zeros((peer_count * buffer_rows + 1, quarter), jnp.bfloat1...  10.1 us
    unnamed x25, local copies, waits for them, and re-layouts  8.83 us
  transfers between devices with their start and end apart: 3, of which 3 were waited for; matrix products, arithmetic and copies ran while one was open for 6% of the time, Pallas kernels for 0%

profile of v1, /device:TPU:1, one launch (start us, length us, event | category | flops | bytes accessed | tf_op | source)
XLA Modules:
  0.0 309.5 jit_solution(16890288595434931676)
XLA Ops:
  6.6 0.8 copy.31
  7.5 0.8 convert_reduce_fusion
  9.0 1.2 fusion.3
  11.0 0.8 copy.32
  14.4 10.1 %scatter_custom_fusion = bf16[1537,512]{1,0:T(8,128)(2,1)S(1)} fusion(s32[1024]{0:T(1024)S(1)} %bitcast.75, bf16[128,512]{1,0:T(8,128)(2,1)S(1)} %constant_dynamic-slice_fusion, s32[1024]{0:T(1024)S(1)} %broadcast_clamp_fusion.1, bf16[]{:T(256)} %constant.114.clone.1), kind=kCustom, calls=%fused_computation.20 | custom fusion | bytes 1573890 | tf_op jit(solution)/shard_map/scatter | solution.py:80
  24.6 52.7 %all_to_all.15 = bf16[64,24,512]{2,1,0:T(8,128)(2,1)S(1)} all-to-all(bf16[64,24,512]{2,1,0:T(8,128)(2,1)S(1)} %bitcast.65), channel_id=1, replica_groups=mesh['dp'=4,'expert'=64] {'expert'}, dimensions={0} | all-to-all | bytes 3145728 | tf_op jit(solution)/shard_map/all_to_all | solution.py:83
  77.4 3.2 %stack.2 = bf16[4,64,24,512]{3,2,1,0:T(8,128)(2,1)} broadcast(bf16[64,24,512]{2,1,0:T(8,128)(2,1)S(1)} %all_to_all.15), dimensions={1,2,3} | broadcast | bytes 7864320 | tf_op jit(solution)/shard_map/stack | solution.py:84
  80.6 5.2 %all-to-all-start.1 = ((bf16[4,64,24,512]{3,2,1,0:T(8,128)(2,1)}), bf16[4,64,24,512]{3,2,1,0:T(8,128)(2,1)}, u32[]{:S(2)}, u32[]{:S(2)}) async-start(bf16[4,64,24,512]{3,2,1,0:T(8,128)(2,1)} %stack.2), calls=%async_computation.1 | async-start | bytes 12582912 | tf_op jit(solution)/shard_map/all_to_all | solution.py:85
  86.4 4.9 %fusion.32 = (bf16[1,2048,2,256]{3,2,1,0:T(2,128)(2,1)S(1)}, bf16[1,2048,2,256]{3,2,1,0:T(2,128)(2,1)S(1)}) fusion(bf16[2,2048,2,256]{3,2,1,0:T(2,128)(2,1)} %param.16), kind=kLoop, calls=%fused_computation.77 | loop fusion | bytes 8388608 | tf_op jit(solution)/shard_map/slice | solution.py:87
  91.3 1.9 copy.42
  93.2 1.9 copy.43
  95.7 61.4 %all-to-all-done.1 = bf16[4,64,24,512]{3,2,1,0:T(8,128)(2,1)} async-done(((bf16[4,64,24,512]{3,2,1,0:T(8,128)(2,1)}), bf16[4,64,24,512]{3,2,1,0:T(8,128)(2,1)}, u32[]{:S(2)}, u32[]{:S(2)}) %all-to-all-start.1) | async-done | bytes 6291488 | tf_op jit(solution)/shard_map/all_to_all | solution.py:85
  157.1 10.9 %copy.39 = bf16[64,24,4,512]{3,2,1,0:T(4,128)(2,1)S(1)} copy(bf16[64,24,4,512]{3,1,0,2:T(8,128)(2,1)} %bitcast.11) | data formatting | bytes 12582912 | tf_op jit(solution)/shard_map/reshape | solution.py:85
  168.0 2.9 copy.41
  171.0 3.4 %fusion.35 = f32[1536,512]{1,0:T(8,128)S(1)} fusion(bf16[1536,2048]{1,0:T(8,128)(2,1)S(1)} %bitcast.63, bf16[2048,512]{1,0:T(8,128)(2,1)S(1)} %bitcast.68), kind=kOutput, calls=%fused_computation.80 | convolution fusion | flops 3221225472 | bytes 11534336 | tf_op jit(solution)/shard_map/dot_general | solution.py:24
  174.4 3.5 %fusion.34 = f32[1536,512]{1,0:T(8,128)S(1)} fusion(bf16[1536,2048]{1,0:T(8,128)(2,1)S(1)} %bitcast.64, bf16[2048,512]{1,0:T(8,128)(2,1)S(1)} %bitcast.67), kind=kOutput, calls=%fused_computation.79 | convolution fusion | flops 3221225472 | bytes 11534336 | tf_op jit(solution)/shard_map/dot_general | solution.py:24
  177.9 1.9 convolution_convert_fusion
  179.8 4.1 %broadcast_select_fusion = bf16[1536,2048]{1,0:T(8,128)(2,1)} fusion(bf16[1536,2048]{1,0:T(8,128)(2,1)S(1)} %convolution_convert_fusion, pred[1536]{0:T(1024)(128)(4,1)S(1)} %fusion.26, bf16[2,256,2048]{2,1,0:T(8,128)(2,1)S(1)} %copy-done.9, f32[1536,512]{1,0:T(8,128)S(1)} %fusion.34), kind=kOutput, calls=%fused_computation.6 | convolution fusion | flops 1619263488 | bytes 16779264 | tf_op jit(solution)/shard_map/dot_general | solution.py:32
  183.9 61.9 %reduce-scatter.2.cloned.1.call-done = bf16[64,24,512]{2,1,0:T(8,128)(2,1)} async-done(((bf16[64,24,2048]{2,1,0:T(8,128)(2,1)}), bf16[64,24,512]{2,1,0:T(8,128)(2,1)}) %reduce-scatter.2.cloned.1.call-update) | async-done | bytes 1572880 | tf_op jit(solution)/shard_map/reduce_scatter | solution.py:93
  245.8 10.6 %all-to-all-start.2 = ((bf16[64,24,512]{2,1,0:T(8,128)(2,1)}), bf16[64,24,512]{2,1,0:T(8,128)(2,1)S(1)}, u32[]{:S(2)}, u32[]{:S(2)}) async-start(bf16[64,24,512]{2,1,0:T(8,128)(2,1)} %reduce-scatter.2.cloned.1.call-done), calls=%async_computation.3 | async-start | bytes 3145728 | tf_op jit(solution)/shard_map/all_to_all | solution.py:94
  257.0 7.0 %gather_fusion.1 = f32[1024]{0:T(1024)S(1)} fusion(f32[128,64]{0,1:T(8,128)S(1)} %fusion.33, s32[1024]{0:T(1024)S(1)} %reshape.276), kind=kCustom, calls=%fused_computation.2 | custom fusion | bytes 16384 | tf_op jit(solution)/shard_map/jit(take_along_axis)/gather | solution.py:62
  264.5 31.7 %all-to-all-done.2 = bf16[64,24,512]{2,1,0:T(8,128)(2,1)S(1)} async-done(((bf16[64,24,512]{2,1,0:T(8,128)(2,1)}), bf16[64,24,512]{2,1,0:T(8,128)(2,1)S(1)}, u32[]{:S(2)}, u32[]{:S(2)}) %all-to-all-start.2) | async-done | bytes 1572896 | tf_op jit(solution)/shard_map/all_to_all | solution.py:94
  296.3 4.0 %gather_fusion = bf16[1024,512]{1,0:T(8,128)(2,1)S(1)} fusion(bf16[1537,512]{1,0:T(8,128)(2,1)S(1)} %concatenate.3, s32[1024]{0:T(1024)S(1)} %broadcast_clamp_fusion), kind=kCustom, calls=%fused_computation.1 | custom fusion | bytes 2101248 | tf_op jit(solution)/shard_map/gather | solution.py:98
  301.0 1.6 add_convert_fusion
  (60 shorter events, 7.2 us)
Async XLA Ops:
  6.5 250.1 %copy-start = (bf16[2048,64]{0,1:T(8,128)(2,1)S(1)}, bf16[2048,64]{0,1:T(8,128)(2,1)}, u32[]{:S(2)}) copy-start(bf16[2048,64]{0,1:T(8,128)(2,1)} %param.11) | copy-start | bytes 786436
  6.5 5.9 %copy-start.7 = (s32[128]{0:T(128)S(1)}, s32[128]{0:T(128)}, u32[]{:S(2)}) copy-start(s32[128]{0:T(128)} %param.14) | copy-start | bytes 1540
  11.9 1.5 copy-start.1
  12.7 0.9 copy-start.8
  13.6 0.8 copy-start.2
  80.6 76.6 %all-to-all-start.1 = ((bf16[4,64,24,512]{3,2,1,0:T(8,128)(2,1)}), bf16[4,64,24,512]{3,2,1,0:T(8,128)(2,1)}, u32[]{:S(2)}, u32[]{:S(2)}) async-start(bf16[4,64,24,512]{3,2,1,0:T(8,128)(2,1)} %stack.2), calls=%async_computation.1 | async-start | bytes 12582912 | tf_op jit(solution)/shard_map/all_to_all | solution.py:85
  85.8 160.0 %reduce-scatter.2.cloned.1.call-start = ((), (), s32[]{:S(2)}) async-start(), calls=%async_computation.4 | async-start | bytes 7864320 | tf_op jit(solution)/shard_map/reduce_scatter | solution.py:93
  168.0 3.0 copy-start.5
  171.0 3.5 %copy-start.4 = (bf16[256,8,2,256]{3,1,2,0:T(8,128)(2,1)S(1)}, bf16[256,8,2,256]{3,1,2,0:T(8,128)(2,1)}, u32[]{:S(2)}) copy-start(bf16[256,8,2,256]{3,1,2,0:T(8,128)(2,1)} %copy.42) | copy-start | bytes 6291460
  174.4 3.5 %copy-start.9 = (bf16[2,256,2048]{2,1,0:T(8,128)(2,1)S(1)}, bf16[2,256,2048]{2,1,0:T(8,128)(2,1)}, u32[]{:S(2)}) copy-start(bf16[2,256,2048]{2,1,0:T(8,128)(2,1)} %param.17) | copy-start | bytes 6291460
  183.9 72.6 %copy-start.6 = (s32[128,8]{0,1:T(8,128)S(1)}, s32[128,8]{0,1:T(8,128)}, u32[]{:S(2)}) copy-start(s32[128,8]{0,1:T(8,128)} %param.12) | copy-start | bytes 12292
  183.9 72.8 %copy-start.3 = (bf16[128,2048]{1,0:T(8,128)(2,1)S(1)}, bf16[128,2048]{1,0:T(8,128)(2,1)}, u32[]{:S(2)}) copy-start(bf16[128,2048]{1,0:T(8,128)(2,1)} %copy-done.2) | copy-start | bytes 1572868
  245.8 50.4 %all-to-all-start.2 = ((bf16[64,24,512]{2,1,0:T(8,128)(2,1)}), bf16[64,24,512]{2,1,0:T(8,128)(2,1)S(1)}, u32[]{:S(2)}, u32[]{:S(2)}) async-start(bf16[64,24,512]{2,1,0:T(8,128)(2,1)} %reduce-scatter.2.cloned.1.call-done), calls=%async_computation.3 | async-start | bytes 3145728 | tf_op jit(solution)/shard_map/all_to_all | solution.py:94
Sparse Core Ops, SparseCore 0:
  184.0 61.7 reduce-scatter.1
